TPU v7x, 32 devices: a whole 2x2x4 slice. The times are simulated.
32 devices in a mesh: dp: 8 (over z, y), tensor: 4 (over x, core).
Axes of the slice: x: 2, y: 2, z: 4, core: 2. Of those that a mesh axis runs over, the one named last changes fastest.
Arguments:
- tokens: bfloat16 [8, 512, 768], P('dp'), may hold values from -6 to 6
- cotangent: bfloat16 [8, 512, 768], P('dp'), may hold values from -6 to 6
- norm_gain: float32 [768], replicated, may hold values from 0.1 to 1.9
- w_z: bfloat16 [768, 1536], P(None, 'tensor'), may hold values from -0.21875 to 0.21875
- w_x: bfloat16 [768, 1536], P(None, 'tensor'), may hold values from -0.21875 to 0.21875
- w_bc: bfloat16 [768, 256], replicated, may hold values from -0.21875 to 0.21875
- w_dt: bfloat16 [768, 24], P(None, 'tensor'), may hold values from -0.21875 to 0.21875
- conv_x: float32 [4, 1536], P(None, 'tensor'), may hold values from -3 to 3
- conv_x_bias: float32 [1536], P('tensor'), may hold values from -3 to 3
- conv_bc: float32 [4, 256], replicated, may hold values from -3 to 3
- conv_bc_bias: float32 [256], replicated, may hold values from -3 to 3
- dt_bias: float32 [24], P('tensor'), may hold values from -5 to -1
- a_log: float32 [24], P('tensor'), may hold values from -4 to 2
- d_skip: float32 [24], P('tensor'), may hold values from 0.5 to 2
- gate_gain: float32 [1536], P('tensor'), may hold values from 0.1 to 1.9
- w_out: bfloat16 [1536, 768], P('tensor'), may hold values from -0.15625 to 0.15625
Outputs:
- result: bfloat16 [8, 512, 768], P('dp')
- grad_x: bfloat16 [8, 512, 768], P('dp')
- grad_norm_gain: float32 [768], replicated
- grad_w_z: float32 [768, 1536], P(None, 'tensor')
- grad_w_x: float32 [768, 1536], P(None, 'tensor')
- grad_w_bc: float32 [768, 256], replicated
- grad_w_dt: float32 [768, 24], P(None, 'tensor')
- grad_conv_x: float32 [4, 1536], P(None, 'tensor')
- grad_conv_x_bias: float32 [1536], P('tensor')
- grad_conv_bc: float32 [4, 256], replicated
- grad_conv_bc_bias: float32 [256], replicated
- grad_dt_bias: float32 [24], P('tensor')
- grad_a_log: float32 [24], P('tensor')
- grad_d_skip: float32 [24], P('tensor')
- grad_gate_gain: float32 [1536], P('tensor')
- grad_w_out: float32 [1536, 768], P('tensor')
All inputs are finite; a program needn't handle non-finite values.
Results may differ from a plain program's by a relative error of at most 0.013.
Values may be sent and summed in bfloat16 or wider, within the bound.
A program may use at most 128 MiB of HBM per device.

v0:
```python
import jax
import jax.numpy as jnp
from jax import lax
from jax.sharding import PartitionSpec as P

Q = 256


epsilon = 1e-05
highest = lax.Precision.HIGHEST


def input_norm(values, norm_gain):
    return (
        values
        * lax.rsqrt(jnp.mean(values * values, axis=-1, keepdims=True) + epsilon)
        * norm_gain[None, :]
    )


def causal_conv(values, kernel, shift_bias):
    length = values.shape[0]
    kernel_taps = kernel.shape[0]
    padded = jnp.pad(values, ((kernel_taps - 1, 0), (0, 0)))
    summed = jnp.zeros_like(values) + shift_bias[None, :]
    for offset in range(kernel_taps):
        summed = summed + kernel[offset][None, :] * padded[offset : offset + length]
    return summed


def state_scan(xheads, b_rows, c_rows, step_size, log_decay):
    length, head_count, head_dim = xheads.shape
    blocks = length // Q
    states = b_rows.shape[1]
    causal_mask = jnp.arange(Q)[:, None] >= jnp.arange(Q)[None, :]

    def advance(carried_state, pieces):
        x_blk, b_blk, c_blk, dt_blk, a_blk = pieces
        cumulative = jnp.cumsum(a_blk, axis=0)
        spread = jnp.where(
            causal_mask[:, :, None], cumulative[:, None, :] - cumulative[None, :, :], -jnp.inf
        )
        scores = jnp.dot(c_blk, b_blk.T, precision=highest)
        mixing = scores[:, :, None] * jnp.exp(spread) * dt_blk[None, :, :]
        inside = jnp.einsum("tsh,shp->thp", mixing, x_blk, precision=highest)
        carried = (
            jnp.einsum("tn,hpn->thp", c_blk, carried_state, precision=highest)
            * jnp.exp(cumulative)[:, :, None]
        )
        weight_tail = jnp.exp(cumulative[-1][None, :] - cumulative) * dt_blk
        update = jnp.einsum(
            "shp,sn->hpn", x_blk * weight_tail[:, :, None], b_blk, precision=highest
        )
        carried_state = carried_state * jnp.exp(cumulative[-1])[:, None, None] + update
        return (carried_state, inside + carried)

    initial = jnp.zeros((head_count, head_dim, states), jnp.float32)
    pieces = (
        xheads.reshape(blocks, Q, head_count, head_dim),
        b_rows.reshape(blocks, Q, states),
        c_rows.reshape(blocks, Q, states),
        step_size.reshape(blocks, Q, head_count),
        log_decay.reshape(blocks, Q, head_count),
    )
    _, outputs = lax.scan(advance, initial, pieces)
    return outputs.reshape(length, head_count, head_dim)


def mixer(
    x_pre, bc_pre, dt_pre, conv_x, conv_x_bias, conv_bc, conv_bc_bias, dt_bias, a_log, d_skip
):
    length, head_count = dt_pre.shape
    xconv = jax.nn.silu(causal_conv(x_pre, conv_x, conv_x_bias))
    bcconv = jax.nn.silu(causal_conv(bc_pre, conv_bc, conv_bc_bias))
    states = bc_pre.shape[1] // 2
    step_size = jax.nn.softplus(dt_pre + dt_bias[None, :])
    log_decay = -step_size * jnp.exp(a_log)[None, :]
    xheads = xconv.reshape(length, head_count, -1)
    mixed = state_scan(xheads, bcconv[:, :states], bcconv[:, states:], step_size, log_decay)
    mixed = mixed + d_skip[None, :, None] * xheads
    return mixed.reshape(length, -1)


def batched_mixer(
    x_pre, bc_pre, dt_pre, conv_x, conv_x_bias, conv_bc, conv_bc_bias, dt_bias, a_log, d_skip
):
    mapped = jax.vmap(mixer, in_axes=(0, 0, 0, None, None, None, None, None, None, None))
    return mapped(
        x_pre, bc_pre, dt_pre, conv_x, conv_x_bias, conv_bc, conv_bc_bias, dt_bias, a_log, d_skip
    )


def silu_slope(values):
    sigmoid = jax.nn.sigmoid(values)
    return sigmoid * (1.0 + values * (1.0 - sigmoid))


def contract_rows(left, right):
    return lax.dot_general(
        left, right, (((0,), (0,)), ((), ())), preferred_element_type=jnp.float32
    )


def contract_cols(left, right):
    return lax.dot_general(
        left, right, (((1,), (1,)), ((), ())), preferred_element_type=jnp.float32
    )


def per_device(
    tokens,
    cotangent,
    norm_gain,
    w_z,
    w_x,
    w_bc,
    w_dt,
    conv_x,
    conv_x_bias,
    conv_bc,
    conv_bc_bias,
    dt_bias,
    a_log,
    d_skip,
    gate_gain,
    w_out,
):
    seq_count, length, width = tokens.shape
    row_count = seq_count * length
    share_rows = row_count // lax.axis_size("tensor")
    first_row = lax.axis_index("tensor") * share_rows
    widef = tokens.reshape(row_count, width).astype(jnp.float32)
    normed = input_norm(widef, norm_gain).astype(jnp.bfloat16)
    gate_pre = jnp.dot(normed, w_z, preferred_element_type=jnp.float32)
    x_pre = jnp.dot(normed, w_x, preferred_element_type=jnp.float32)
    bc_pre = jnp.dot(normed, w_bc, preferred_element_type=jnp.float32)
    dt_pre = jnp.dot(normed, w_dt, preferred_element_type=jnp.float32)
    mixed, mixer_back = jax.vjp(
        batched_mixer,
        x_pre.reshape(seq_count, length, -1),
        bc_pre.reshape(seq_count, length, -1),
        dt_pre.reshape(seq_count, length, -1),
        conv_x,
        conv_x_bias,
        conv_bc,
        conv_bc_bias,
        dt_bias,
        a_log,
        d_skip,
    )
    mixed = mixed.reshape(row_count, -1)
    inner_total = mixed.shape[1] * lax.axis_size("tensor")
    gate_act = jax.nn.silu(gate_pre)
    gated = mixed * gate_act
    squares = lax.psum(jnp.sum(gated * gated, axis=-1), "tensor")
    inverse = lax.rsqrt(squares / inner_total + epsilon)[:, None]
    gated_n = (gated * inverse * gate_gain[None, :]).astype(jnp.bfloat16)
    partial_out = jnp.dot(gated_n, w_out, preferred_element_type=jnp.float32)
    summed_out = lax.psum(partial_out.astype(jnp.bfloat16), "tensor").astype(jnp.float32)
    result = (widef + summed_out).astype(jnp.bfloat16)
    result = result.reshape(seq_count, length, width)
    cotan = cotangent.reshape(row_count, width)
    grad_w_out = contract_rows(gated_n, cotan)
    d_gated_n = contract_cols(cotan, w_out)
    grad_gate_gain = jnp.sum(d_gated_n * gated * inverse, axis=0)
    scaled = gate_gain[None, :] * d_gated_n
    products = lax.psum(jnp.sum(scaled * gated, axis=-1), "tensor")
    d_gated = inverse * scaled - gated * inverse**3 * (products / inner_total)[:, None]
    d_mixed = d_gated * gate_act
    d_gate_pre = d_gated * mixed * silu_slope(gate_pre)
    back = mixer_back(d_mixed.reshape(seq_count, length, -1))
    d_gate_b = d_gate_pre.astype(jnp.bfloat16)
    d_x_b = back[0].reshape(row_count, -1).astype(jnp.bfloat16)
    d_bc_b = back[1].reshape(row_count, -1).astype(jnp.bfloat16)
    d_dt_b = back[2].reshape(row_count, -1).astype(jnp.bfloat16)
    grad_w_z = contract_rows(normed, d_gate_b)
    grad_w_x = contract_rows(normed, d_x_b)
    grad_w_bc = contract_rows(normed, d_bc_b)
    grad_w_dt = contract_rows(normed, d_dt_b)
    d_normed_part = (
        contract_cols(d_gate_b, w_z)
        + contract_cols(d_x_b, w_x)
        + contract_cols(d_bc_b, w_bc)
        + contract_cols(d_dt_b, w_dt)
    )
    input_rows = lax.dynamic_slice_in_dim(widef, first_row, share_rows, 0)
    _, share_back = jax.vjp(input_norm, input_rows, norm_gain)
    d_normed = lax.psum(d_normed_part.astype(jnp.bfloat16), "tensor").astype(jnp.float32)
    _, full_back = jax.vjp(input_norm, widef, norm_gain)
    d_tokens, _ = full_back(d_normed)
    d_normed_rows = lax.dynamic_slice_in_dim(d_normed, first_row, share_rows, 0)
    _, grad_norm_gain = share_back(d_normed_rows)
    grad_x = (cotan.astype(jnp.float32) + d_tokens).astype(jnp.bfloat16)
    grad_x = grad_x.reshape(seq_count, length, width)
    grad_w_bc, grad_conv_bc, grad_conv_bc_bias, grad_norm_gain = lax.psum(
        (grad_w_bc, back[5], back[6], grad_norm_gain), ("dp", "tensor")
    )
    reduced = lax.psum(
        (
            grad_w_z,
            grad_w_x,
            grad_w_dt,
            back[3],
            back[4],
            back[7],
            back[8],
            back[9],
            grad_gate_gain,
            grad_w_out,
        ),
        "dp",
    )
    (
        grad_w_z,
        grad_w_x,
        grad_w_dt,
        grad_conv_x,
        grad_conv_x_bias,
        grad_dt_bias,
        grad_a_log,
        grad_d_skip,
        grad_gate_gain,
        grad_w_out,
    ) = reduced
    return (
        result,
        grad_x,
        grad_norm_gain,
        grad_w_z,
        grad_w_x,
        grad_w_bc,
        grad_w_dt,
        grad_conv_x,
        grad_conv_x_bias,
        grad_conv_bc,
        grad_conv_bc_bias,
        grad_dt_bias,
        grad_a_log,
        grad_d_skip,
        grad_gate_gain,
        grad_w_out,
    )


def solution(mesh):
    placed = (
        P("dp", None, None),
        P("dp", None, None),
        P(),
        P(None, "tensor"),
        P(None, "tensor"),
        P(),
        P(None, "tensor"),
        P(None, "tensor"),
        P("tensor"),
        P(),
        P(),
        P("tensor"),
        P("tensor"),
        P("tensor"),
        P("tensor"),
        P("tensor", None),
    )
    return jax.shard_map(
        per_device,
        mesh=mesh,
        in_specs=placed,
        out_specs=(
            P("dp", None, None),
            P("dp", None, None),
            P(),
            P(None, "tensor"),
            P(None, "tensor"),
            P(),
            P(None, "tensor"),
            P(None, "tensor"),
            P("tensor"),
            P(),
            P(),
            P("tensor"),
            P("tensor"),
            P("tensor"),
            P("tensor"),
            P("tensor", None),
        ),
        check_vma=False,
    )
```

profile of v0, /device:TPU:0, one launch (start us, length us, event | category | flops | bytes accessed | tf_op | source)
XLA Modules:
  0.0 580.4 jit_solution(8823095844115345862)
XLA Ops:
  7.4 1.4 fusion.140
  9.7 1.7 fusion.186
  13.8 1.6 fusion.158
  15.5 1.4 copy.191
  16.9 1.4 reshape.1072
  23.5 54.7 %while.71 = (s32[]{:T(128)}, f32[1,6,64,128]{3,2,1,0:T(8,128)S(1)}, f32[2,1,256,6,64]{2,0,4,3,1:T(2,128)}, f32[2,1,128,256]{2,3,1,0:T(8,128)}, f32[2,1,256,256,6...) while((s32[]{:T(128)}, f32[1,6,64,128]{3,2,1,0:T(8,128)S(1)}, ...), condition=%wide.region_4.5_spmd.clone.clone, body=%wide.region_1.4_spmd.clone.clone.sunk | while | flops 708627456 | bytes 15328889 | solution.py:65
  24.2 1.8 reduce-window.48
  28.7 2.6 multiply_dynamic-update-slice_fusion.4
  34.4 1.9 fusion.284
  36.7 9.0 %dynamic_update_slice.218 = f32[2,1,256,6,64]{2,0,4,3,1:T(2,128)} dynamic-update-slice(f32[2,1,256,6,64]{2,0,4,3,1:T(2,128)} %get-tuple-element.1940, f32[1,1,256,6,64]{2,0,4,3,1:T(1,128)S(1)} %copy.365, s32[]{:T(128)} %get-tuple-element.1938, s32[]{:T(128)} %constant.179.clone.1..sunk.1, s32[]{:T(128)} %constant.179.clone.1..sunk.1, s32[]{:T(128)} %constant.179.clone.1..sunk.1, ...) | dynamic-update-slice | bytes 786436 | tf_op jit(solution)/shard_map/jvp(vmap())/while/body/jit(dynamic_update_index_in_dim)/dynamic_update_slice | solution.py:65
  51.5 1.8 reduce-window.48
  56.0 2.7 multiply_dynamic-update-slice_fusion.4
  61.8 1.9 fusion.284
  64.1 9.0 %dynamic_update_slice.218 = f32[2,1,256,6,64]{2,0,4,3,1:T(2,128)} dynamic-update-slice(f32[2,1,256,6,64]{2,0,4,3,1:T(2,128)} %get-tuple-element.1940, f32[1,1,256,6,64]{2,0,4,3,1:T(1,128)S(1)} %copy.365, s32[]{:T(128)} %get-tuple-element.1938, s32[]{:T(128)} %constant.179.clone.1..sunk.1, s32[]{:T(128)} %constant.179.clone.1..sunk.1, s32[]{:T(128)} %constant.179.clone.1..sunk.1, ...) | dynamic-update-slice | bytes 786436 | tf_op jit(solution)/shard_map/jvp(vmap())/while/body/jit(dynamic_update_index_in_dim)/dynamic_update_slice | solution.py:65
  78.1 2.1 copy.268
  80.2 2.3 copy.197
  82.7 3.4 multiply_reduce_fusion.6
  86.1 9.0 %psum.126 = f32[512]{0:T(512)} all-reduce(f32[512]{0:T(512)S(1)} %get-tuple-element.1483), channel_id=1, replica_groups=mesh['dp'=8,'tensor'=4] {'tensor'}, use_global_device_ids=true, to_apply=%region_6.7 | all-reduce | flops 512 | bytes 4096 | tf_op jit(solution)/shard_map/psum | solution.py:155
  95.9 2.8 convolution_convert_fusion
  98.7 2.1 multiply_reduce_fusion
  100.8 6.0 %psum.128 = f32[512]{0:T(512)S(1)} all-reduce(f32[512]{0:T(512)} %get-tuple-element.1335), channel_id=1, replica_groups=mesh['dp'=8,'tensor'=4] {'tensor'}, use_global_device_ids=true, to_apply=%region_9.10 | all-reduce | flops 512 | bytes 4096 | tf_op jit(solution)/shard_map/psum | solution.py:167
  106.8 4.1 fusion.156
  110.9 1.4 copy.198
  112.4 1.4 reshape_reshape.4
  117.5 114.6 %while.70 = (s32[]{:T(128)}, f32[1,6,64,128]{3,2,1,0:T(8,128)S(1)}, f32[2,1,256,6,64]{2,0,4,3,1:T(2,128)}, f32[2,1,256,128]{3,2,1,0:T(8,128)}, f32[2,1,256,128]{...) while((s32[]{:T(128)}, f32[1,6,64,128]{3,2,1,0:T(8,128)S(1)}, ...), condition=%wide.region_21.22_spmd.clone, body=%wide.region_10.21_spmd.clone.sunk | while | flops 1414609920 | bytes 22201356 | solution.py:65
  117.5 1.6 constant_dynamic-slice_fusion.15
  120.7 4.7 fusion.270
  125.9 1.3 constant_dynamic-slice_fusion.17
  128.6 1.3 copy.357
  130.5 1.3 copy.358
  134.3 1.4 fusion.277
  137.1 8.8 %reduce-window.46 = f32[1,6,2,128]{3,2,1,0:T(2,128)} reduce-window(f32[1,6,2,128]{3,2,1,0:T(2,128)} %bitcast.662, f32[]{:T(128)} %constant.180.clone.1..sunk), window={size=1x1x1x128 pad=0_0x0_0x0_0x0_127}, to_apply=%region_19.19 | reduce-window | flops 195072 | bytes 12292 | tf_op jit(solution)/shard_map/reduce-window.18
  145.9 1.3 copy.359
  149.7 1.4 copy.360
  153.1 1.3 dynamic_update_slice.209
  154.5 1.3 constant_dynamic-slice_fusion.16
  155.8 2.5 fusion.269
  158.7 9.0 %dynamic_update_slice.208 = f32[2,1,256,6,64]{2,0,4,3,1:T(2,128)} dynamic-update-slice(f32[2,1,256,6,64]{2,0,4,3,1:T(2,128)} %get-tuple-element.2025, f32[1,1,256,6,64]{2,0,4,3,1:T(1,128)S(1)} %copy.356, s32[]{:T(128)S(6)} %sub.180, s32[]{:T(128)} %constant.179.clone.1..sunk, s32[]{:T(128)} %constant.179.clone.1..sunk, s32[]{:T(128)} %constant.179.clone.1..sunk, s32[]{:T(128)} %constant.179.clone.1..sunk) | dynamic-update-slice | bytes 786436 | tf_op jit(solution)/shard_map/transpose(jvp(vmap()))/while/body/jit(dynamic_update_index_in_dim)/dynamic_update_slice | solution.py:65
  169.3 2.0 fusion.272
  174.8 1.6 constant_dynamic-slice_fusion.15
  178.0 4.7 fusion.270
  183.2 1.3 constant_dynamic-slice_fusion.17
  191.6 1.4 fusion.277
  194.3 8.8 %reduce-window.46 = f32[1,6,2,128]{3,2,1,0:T(2,128)} reduce-window(f32[1,6,2,128]{3,2,1,0:T(2,128)} %bitcast.662, f32[]{:T(128)} %constant.180.clone.1..sunk), window={size=1x1x1x128 pad=0_0x0_0x0_0x0_127}, to_apply=%region_19.19 | reduce-window | flops 195072 | bytes 12292 | tf_op jit(solution)/shard_map/reduce-window.18
  203.1 1.3 copy.359
  207.0 1.4 copy.360
  210.4 1.3 dynamic_update_slice.209
  211.7 1.3 constant_dynamic-slice_fusion.16
  213.1 2.5 fusion.269
  216.0 9.0 %dynamic_update_slice.208 = f32[2,1,256,6,64]{2,0,4,3,1:T(2,128)} dynamic-update-slice(f32[2,1,256,6,64]{2,0,4,3,1:T(2,128)} %get-tuple-element.2025, f32[1,1,256,6,64]{2,0,4,3,1:T(1,128)S(1)} %copy.356, s32[]{:T(128)S(6)} %sub.180, s32[]{:T(128)} %constant.179.clone.1..sunk, s32[]{:T(128)} %constant.179.clone.1..sunk, s32[]{:T(128)} %constant.179.clone.1..sunk, s32[]{:T(128)} %constant.179.clone.1..sunk) | dynamic-update-slice | bytes 786436 | tf_op jit(solution)/shard_map/transpose(jvp(vmap()))/while/body/jit(dynamic_update_index_in_dim)/dynamic_update_slice | solution.py:65
  226.6 2.0 fusion.272
  232.2 2.2 copy.269
  234.4 2.3 copy.212
  236.7 2.1 multiply_reduce_fusion.3
  247.4 1.4 fusion.178
  248.9 1.7 fusion.180
  250.6 1.7 fusion.182
  252.3 1.6 fusion.151
  257.0 38.6 %all-reduce.23 = (f32[768,6]{0,1:T(8,128)}, f32[4,384]{1,0:T(4,128)}, f32[384]{0:T(512)}, f32[6]{0:T(128)}, f32[6]{0:T(128)}, /*index=5*/f32[6]{0:T(128)}, f32[384]{0:T(512)}) all-reduce(f32[768,6]{0,1:T(8,128)S(1)} %fusion.173, f32[4,384]{1,0:T(4,128)S(1)} %pad_add_fusion.6, ...), channel_id=1, replica_groups=mesh['dp'=8,'tensor'=4] {'dp'}, use_global_device_ids=true, to_apply=%region_30.31 | all-reduce | flops 6930 | bytes 55440 | tf_op jit(solution)/shard_map/psum | solution.py:198
  298.1 37.1 %all-reduce.22 = (f32[768]{0:T(1024)}, f32[4,256]{1,0:T(4,128)}, f32[256]{0:T(256)}) all-reduce(f32[768]{0:T(1024)S(1)} %fusion.166, f32[4,256]{1,0:T(4,128)S(1)} %pad_add_fusion.7, f32[256]{0:T(256)S(1)} %get-tuple-element.1344), channel_id=1, replica_groups=mesh['dp'=8,'tensor'=4] {'dp','tensor'}, use_global_device_ids=true, to_apply=%region_26.27 | all-reduce | flops 2048 | bytes 16384 | tf_op jit(solution)/shard_map/psum | solution.py:195
  335.6 3.2 fusion.149
  338.7 86.3 %all-reduce.30.cloned.1.call-done = f32[768,256]{1,0:T(8,128)} async-done(((f32[768,256]{1,0:T(8,128)}), f32[768,256]{1,0:T(8,128)}) %all-reduce.30.cloned.1.call-update) | async-done | bytes 786448 | tf_op jit(solution)/shard_map/psum | solution.py:195
  425.1 142.8 %all-reduce.32.cloned.1.call-done = (f32[768,384]{1,0:T(8,128)}, f32[768,384]{1,0:T(8,128)}, f32[384,768]{1,0:T(8,128)}) async-done(((f32[768,384]{1,0:T(8,128)}, f32[768,384]{1,0:T(8,128)}, f32[384,768]{1,0:T(8,128)}), (f32[768,384]{1,0:T(8,128)}, f32[768,384]{1,0:T(8,128)}, f32[384,768]{1,0:T(8,128)})) %all-reduce.32.cloned.1.call-update) | async-done | bytes 3538960 | tf_op jit(solution)/shard_map/psum | solution.py:198
  567.9 2.5 copy.471
  (420 shorter events, 92.8 us)
Async XLA Ops:
  7.2 75.5 %copy-start = (bf16[768,384]{1,0:T(8,128)(2,1)S(1)}, bf16[768,384]{1,0:T(8,128)(2,1)}, u32[]{:S(2)}) copy-start(bf16[768,384]{1,0:T(8,128)(2,1)} %param.23) | copy-start | bytes 1769476
  7.2 4.2 copy-start.89
  7.2 288.5 %all-reduce.34.cloned.1.call-start = ((), (), s32[]{:S(2)}) async-start(), calls=%async_computation.2 | async-start | bytes 3145728 | tf_op jit(solution)/shard_map/psum | solution.py:159
  8.8 10.7 %copy-start.83 = (f32[512]{0:T(512)}, f32[512]{0:T(512)S(1)}, u32[]{:S(2)}) copy-start(f32[512]{0:T(512)S(1)} %fusion.176) | copy-start | bytes 6148
  9.7 2.9 copy-start.74
  9.7 2.9 copy-start.76
  9.7 2.9 copy-start.78
  9.7 2.9 copy-start.80
  16.9 2.6 copy-start.72
  19.6 3.9 copy-start.90
  23.5 7.8 %copy-start.28 = (f32[2,1,256,6]{2,3,1,0:T(8,128)}, f32[2,1,256,6]{2,3,1,0:T(8,128)S(1)}, u32[]{:S(2)}) copy-start(f32[2,1,256,6]{2,3,1,0:T(8,128)S(1)} %get-tuple-element.1985) | copy-start | bytes 36868 | tf_op jit(solution)/shard_map/jvp(vmap())/while
  45.7 2.8 copy-start.33
  45.7 2.8 copy-start.39
  45.7 2.9 copy-start.32
  45.7 2.9 copy-start.41
  45.7 2.9 copy-start.43
  45.7 3.0 copy-start.38
  45.7 3.0 copy-start.52
  45.7 4.2 copy-start.34
  45.7 4.2 copy-start.45
  45.7 4.3 copy-start.19
  45.8 5.0 copy-start.29
  50.7 7.9 %copy-start.28 = (f32[2,1,256,6]{2,3,1,0:T(8,128)}, f32[2,1,256,6]{2,3,1,0:T(8,128)S(1)}, u32[]{:S(2)}) copy-start(f32[2,1,256,6]{2,3,1,0:T(8,128)S(1)} %get-tuple-element.1985) | copy-start | bytes 36868 | tf_op jit(solution)/shard_map/jvp(vmap())/while
  73.1 2.8 copy-start.33
  73.1 2.8 copy-start.39
  73.1 2.9 copy-start.32
  73.1 2.9 copy-start.41
  73.1 2.9 copy-start.43
  73.1 3.0 copy-start.38
  73.1 3.0 copy-start.52
  73.1 4.2 copy-start.34
  73.1 4.2 copy-start.45
  73.1 4.3 copy-start.19
  73.1 5.0 copy-start.29
  78.1 4.4 copy-start.30
  78.1 4.4 copy-start.92
  78.1 4.6 copy-start.69
  78.1 4.6 copy-start.84
  82.7 24.1 %copy-start.56 = (f32[384]{0:T(512)}, f32[384]{0:T(512)S(1)}, u32[]{:S(2)}) copy-start(f32[384]{0:T(512)S(1)} %mul.847) | copy-start | bytes 4612
  82.7 13.2 %copy-start.54 = (f32[384]{0:T(512)S(1)}, f32[384]{0:T(512)}, u32[]{:S(2)}) copy-start(f32[384]{0:T(512)} %param.34) | copy-start | bytes 4612
  86.1 12.6 %copy-start.3 = (f32[512,384]{1,0:T(8,128)S(1)}, f32[512,384]{1,0:T(8,128)}, u32[]{:S(2)}) copy-start(f32[512,384]{1,0:T(8,128)} %get-tuple-element.1484) | copy-start | bytes 2359300
  86.1 12.6 %copy-start.15 = (bf16[384,768]{1,0:T(8,128)(2,1)S(1)}, bf16[384,768]{1,0:T(8,128)(2,1)}, u32[]{:S(2)}) copy-start(bf16[384,768]{1,0:T(8,128)(2,1)} %param.35) | copy-start | bytes 1769476
  95.1 3.6 copy-start.11
  95.9 11.0 %copy-start.49 = (f32[512]{0:T(512)}, f32[512]{0:T(512)S(1)}, u32[]{:S(2)}) copy-start(f32[512]{0:T(512)S(1)} %get-tuple-element.1530) | copy-start | bytes 6148
  112.3 5.1 copy-start.7
  117.5 7.9 %copy-start.16 = (pred[256,256]{1,0:T(8,128)(4,1)}, pred[256,256]{1,0:T(8,128)(4,1)S(1)}, u32[]{:S(2)}) copy-start(pred[256,256]{1,0:T(8,128)(4,1)S(1)} %get-tuple-element.2081) | copy-start | bytes 196612 | tf_op jit(solution)/shard_map/transpose(jvp(vmap()))/while
  167.7 5.5 copy-start.14
  167.7 5.5 copy-start.24
  167.7 6.4 %copy-start.96 = (f32[2,1,6,1,1]{2,4,3,1,0:T(1,128)S(1)}, f32[2,1,6,1,1]{2,4,3,1,0:T(1,128)}, u32[]{:S(2)}) copy-start(f32[2,1,6,1,1]{2,4,3,1,0:T(1,128)} %get-tuple-element.2061) | copy-start | bytes 148 | tf_op jit(solution)/shard_map/transpose(jvp(vmap()))/while
  169.3 5.5 copy-start.17
  174.8 7.9 %copy-start.16 = (pred[256,256]{1,0:T(8,128)(4,1)}, pred[256,256]{1,0:T(8,128)(4,1)S(1)}, u32[]{:S(2)}) copy-start(pred[256,256]{1,0:T(8,128)(4,1)S(1)} %get-tuple-element.2081) | copy-start | bytes 196612 | tf_op jit(solution)/shard_map/transpose(jvp(vmap()))/while
  224.9 5.5 copy-start.14
  224.9 5.5 copy-start.24
  224.9 6.4 %copy-start.96 = (f32[2,1,6,1,1]{2,4,3,1,0:T(1,128)S(1)}, f32[2,1,6,1,1]{2,4,3,1,0:T(1,128)}, u32[]{:S(2)}) copy-start(f32[2,1,6,1,1]{2,4,3,1,0:T(1,128)} %get-tuple-element.2061) | copy-start | bytes 148 | tf_op jit(solution)/shard_map/transpose(jvp(vmap()))/while
  226.5 5.5 copy-start.17
  232.2 4.5 copy-start.6
  232.2 4.5 copy-start.13
  232.2 4.5 copy-start.57
  246.3 178.8 %all-reduce.30.cloned.1.call-start = ((), (), s32[]{:S(2)}) async-start(), calls=%async_computation | async-start | bytes 1572864 | tf_op jit(solution)/shard_map/psum | solution.py:195
  248.8 319.1 %all-reduce.32.cloned.1.call-start = ((), (), s32[]{:S(2)}) async-start(), calls=%async_computation.1 | async-start | bytes 7077888 | tf_op jit(solution)/shard_map/psum | solution.py:198
  254.0 2.7 copy-start.95
  254.0 3.0 copy-start.86
  295.7 39.6 %copy-start.10 = (bf16[512,768]{1,0:T(8,128)(2,1)S(1)}, bf16[512,768]{1,0:T(8,128)(2,1)}, u32[]{:S(2)}) copy-start(bf16[512,768]{1,0:T(8,128)(2,1)} %get-tuple-element.1468) | copy-start | bytes 2359300
  297.0 38.6 %copy-start.59 = (f32[512]{0:T(512)S(1)}, f32[512]{0:T(512)}, u32[]{:S(2)}) copy-start(f32[512]{0:T(512)} %copy-done.58) | copy-start | bytes 6148
  (61 other events, 87.6 us)
Sparse Core Ops, SparseCore 0:
  246.4 43.3 all-reduce.33
  295.0 130.0 all-reduce.29
  430.1 137.7 all-reduce.31
where the time goes:
time: 585 us; the launch traced here: 580 us
  waiting for transfers between devices  229 us (39%)
  local copies, waits for them, and re-layouts  118 us (20%)
  blocking collectives  90.8 us (16%)
  other arithmetic  71.2 us (12%)
  matrix products  55.8 us (10%)
  between operations  14.7 us (3%)
    psum x1, waiting for transfers between devices, per_device(): lax.psum((grad_w_z, grad_w_x, grad_w_dt, back[3], back[4], back[7], back[...  143 us
    psum x1, waiting for transfers between devices, per_device(): lax.psum((grad_w_bc, back[5], back[6], grad_norm_gain), ('dp', 'tensor'))  86.3 us
    dynamic_update_slice x26, local copies, waits for them, and re-layouts, state_scan(): _, outputs = lax.scan(advance, initial, pieces)  44.2 us
    psum x1, blocking collectives, per_device(): lax.psum((grad_w_z, grad_w_x, grad_w_dt, back[3], back[4], back[7], back[...  38.6 us
    psum x1, blocking collectives, per_device(): lax.psum((grad_w_bc, back[5], back[6], grad_norm_gain), ('dp', 'tensor'))  37.1 us
    another operation x19, other arithmetic  26.8 us
    another operation x28, local copies, waits for them, and re-layouts  18.7 us
    dot_general x6, matrix products, advance(): inside = jnp.einsum('tsh,shp->thp', mixing, x_blk, precision=highest)  18.1 us
  transfers between devices with their start and end apart: 3, of which 2 were waited for; matrix products, arithmetic and copies ran while one was open for 3% of the time, Pallas kernels for 0%

commit v1 on v0

v1 whole, which is shorter than its diff:
```python
import functools

import jax
import jax.numpy as jnp
from jax import lax
from jax.experimental import pallas as pl
from jax.experimental.pallas import tpu as pltpu
from jax.sharding import PartitionSpec as P

Q = 256
LANES = 128
HEAD = 8
epsilon = 1e-05
highest = lax.Precision.HIGHEST
f32 = jnp.float32
bf16 = jnp.bfloat16
NN = ((1,), (0,))
NT = ((1,), (1,))
TN = ((0,), (0,))


def mm(a, b, dims=NN):
    return lax.dot_general(
        a.astype(bf16), b.astype(bf16), (dims, ((), ())), preferred_element_type=f32
    )


def exact(a, b, dims=NN):
    return lax.dot_general(a, b, (dims, ((), ())), precision=highest, preferred_element_type=f32)


def iota(shape, dim):
    return lax.broadcasted_iota(jnp.int32, shape, dim)


def spread_matrix(width, head_dim):
    return (iota((LANES, width), 1) // head_dim == iota((LANES, width), 0)).astype(f32)


def spread_rows(width, head_dim):
    return (iota((width, LANES), 0) // head_dim == iota((width, LANES), 1)).astype(f32)


def shifted(pad_ref, start, kernel_ref, bias_ref):
    taps = kernel_ref.shape[0]
    total = bias_ref[...] + jnp.zeros((Q, pad_ref.shape[1]), f32)
    for j in range(taps):
        total = total + kernel_ref[j : j + 1, :] * pad_ref[pl.ds(HEAD + start - taps + 1 + j, Q), :]
    return total


def softplus(v):
    return jnp.maximum(v, 0.0) + jnp.log1p(jnp.exp(-jnp.abs(v)))


def decays(dt_rows, hp_ref):
    pre = dt_rows + hp_ref[0:1, :]
    step = softplus(pre)
    rate = jnp.exp(hp_ref[1:2, :])
    log_decay = -step * rate
    lower = (iota((Q, Q), 0) >= iota((Q, Q), 1)).astype(f32)
    return pre, step, rate, log_decay, exact(lower, log_decay)


def kernel_front(
    heads, tok, cot, ng, wz, wx, wbd, cx, cxb, cbc, cbcb, hp, gg, wo,
    normed_o, gate_o, x_o, bc_o, dt_o, cum_o, state_o, mixed_o, dgn_o, stats_o,
):
    length, inner = mixed_o.shape
    states = cbc.shape[1] // 2
    head_dim = inner // heads
    per = LANES // head_dim
    spread = spread_matrix(inner, head_dim)
    x_o[0:HEAD, :] = jnp.zeros((HEAD, inner), f32)
    bc_o[0:HEAD, :] = jnp.zeros((HEAD, 2 * states), f32)
    causal = iota((Q, Q), 0) >= iota((Q, Q), 1)
    lane = iota((Q, LANES), 1)
    chunks = length // Q
    for c in range(chunks):
        rows = pl.ds(c * Q, Q)
        t = tok[rows, :].astype(f32)
        n = t * lax.rsqrt(jnp.mean(t * t, axis=-1, keepdims=True) + epsilon) * ng[...]
        n = n.astype(bf16)
        normed_o[rows, :] = n
        gate_o[rows, :] = mm(n, wz[...])
        x_o[pl.ds(HEAD + c * Q, Q), :] = mm(n, wx[...])
        bd = mm(n, wbd[...])
        bc_o[pl.ds(HEAD + c * Q, Q), :] = bd[:, : 2 * states]
        dt_o[rows, :] = bd[:, 2 * states :]
        dgn_o[rows, :] = mm(cot[rows, :], wo[...], NT)
    state_o[0] = jnp.zeros((inner, states), f32)
    for c in range(chunks):
        rows = pl.ds(c * Q, Q)
        v = shifted(x_o, c * Q, cx, cxb)
        xc = v * jax.nn.sigmoid(v)
        v = shifted(bc_o, c * Q, cbc, cbcb)
        bcc = v * jax.nn.sigmoid(v)
        b = bcc[:, :states].astype(bf16)
        cc = bcc[:, states:].astype(bf16)
        _, step, _, _, cum = decays(dt_o[rows, :], hp)
        cum_o[rows, :] = cum
        cum_t = jnp.transpose(cum)
        u = xc * exact(step, spread)
        scores = mm(cc, b, NT)
        outs = []
        for g in range(inner // LANES):
            part = u[:, g * LANES : (g + 1) * LANES]
            acc = jnp.zeros((Q, LANES), f32)
            for k in range(per):
                h = g * per + k
                e = jnp.exp(jnp.where(causal, cum[:, h : h + 1] - cum_t[h : h + 1, :], -1e30))
                acc = acc + mm(scores * e, jnp.where(lane // head_dim == k, part, 0.0))
            outs.append(acc)
        mixed = jnp.concatenate(outs, axis=1)
        if c > 0:
            mixed = mixed + mm(cc, state_o[c], NT) * exact(jnp.exp(cum), spread)
        if c + 1 < chunks:
            last = cum[Q - 1 : Q, :]
            tail = u * exact(jnp.exp(last - cum), spread)
            update = mm(tail, b, TN)
            if c > 0:
                rowdec = jnp.sum(
                    spread_rows(inner, head_dim) * jnp.exp(last), axis=1, keepdims=True
                )
                update = update + state_o[c] * rowdec
            state_o[c + 1] = update
        skip = jnp.sum(spread * hp_skip_col(hp), axis=0, keepdims=True)
        mixed = mixed + skip * xc
        mixed_o[rows, :] = mixed
        gate = gate_o[rows, :]
        gated = mixed * (gate * jax.nn.sigmoid(gate))
        sq = jnp.sum(gated * gated, axis=1, keepdims=True)
        pr = jnp.sum(gg[...] * dgn_o[rows, :] * gated, axis=1, keepdims=True)
        both = jnp.where(lane == 0, sq, jnp.where(lane == 1, pr, 0.0))
        stats_o[:, c * Q : (c + 1) * Q] = jnp.transpose(both)[0:8, :]


def hp_skip_col(hp):
    wide = jnp.where(iota((LANES, LANES), 0) == iota((LANES, LANES), 1), hp[2:3, :], 0.0)
    return jnp.sum(wide, axis=1, keepdims=True)


def put_rows(ref, start, value):
    count = value.shape[1] // LANES
    for r in range(value.shape[0]):
        for k in range(count):
            at = start + r * count + k
            ref[at : at + 1, :] = value[r : r + 1, k * LANES : (k + 1) * LANES]
    return start + value.shape[0] * count


def kernel_back(
    heads, inner_total, tok, cot, ng, wz, wx, wbd, cx, cxb, cbc, cbcb, hp, gg, wo,
    normed, gate_r, x_r, bc_r, dt_r, cum_r, state_r, mixed_r, dgn_r, stats,
    res_o, dn_o, gz_o, gx_o, gwo_o, gbc_o, sm_o, smt_o,
    gn_s, dz_s, dx_s, dbd_s, dvx_s, dvbc_s, inv_s,
):
    length, inner = mixed_r.shape
    states = cbc.shape[1] // 2
    head_dim = inner // heads
    per = LANES // head_dim
    taps = cx.shape[0]
    spread = spread_matrix(inner, head_dim)
    spread_r = spread_rows(inner, head_dim)
    causal = iota((Q, Q), 0) >= iota((Q, Q), 1)
    lower = causal.astype(f32)
    lane = iota((Q, LANES), 1)
    skip = jnp.sum(spread * hp_skip_col(hp), axis=0, keepdims=True)
    dvx_s[pl.ds(length, HEAD), :] = jnp.zeros((HEAD, inner), f32)
    dvbc_s[pl.ds(length, HEAD), :] = jnp.zeros((HEAD, 2 * states), f32)
    chunks = length // Q
    for c in range(chunks):
        block = jnp.concatenate(
            [stats[:, c * Q : (c + 1) * Q], jnp.zeros((LANES - 8, Q), f32)], axis=0
        )
        inv_s[pl.ds(c * Q, Q), :] = jnp.transpose(block)
    g_gain = jnp.zeros((1, inner), f32)
    g_skip = jnp.zeros((1, inner), f32)
    g_alog = jnp.zeros((1, LANES), f32)
    g_dtb = jnp.zeros((1, LANES), f32)
    g_cx = [jnp.zeros((1, inner), f32) for _ in range(taps)]
    g_cxb = jnp.zeros((1, inner), f32)
    g_cbc = [jnp.zeros((1, 2 * states), f32) for _ in range(taps)]
    g_cbcb = jnp.zeros((1, 2 * states), f32)
    d_state = None
    for c in reversed(range(chunks)):
        rows = pl.ds(c * Q, Q)
        gate = gate_r[rows, :]
        mixed = mixed_r[rows, :]
        sg = jax.nn.sigmoid(gate)
        act = gate * sg
        gated = mixed * act
        inv = lax.rsqrt(inv_s[rows, :][:, 0:1] / inner_total + epsilon)
        pm = inv_s[rows, :][:, 1:2] / inner_total
        dgn = dgn_r[rows, :]
        normal = gated * inv
        gn_s[rows, :] = (normal * gg[...]).astype(bf16)
        g_gain = g_gain + jnp.sum(dgn * normal, axis=0, keepdims=True)
        dg = inv * (gg[...] * dgn) - gated * (inv * inv * inv) * pm
        dy = dg * act
        dz_s[rows, :] = (dg * mixed * (sg * (1.0 + gate * (1.0 - sg)))).astype(bf16)

        vx = shifted(x_r, c * Q, cx, cxb)
        sx = jax.nn.sigmoid(vx)
        xc = vx * sx
        vb = shifted(bc_r, c * Q, cbc, cbcb)
        sb = jax.nn.sigmoid(vb)
        bcc = vb * sb
        b = bcc[:, :states].astype(bf16)
        cc = bcc[:, states:].astype(bf16)
        pre = dt_r[rows, :] + hp[0:1, :]
        step = softplus(pre)
        rate = jnp.exp(hp[1:2, :])
        log_decay = -step * rate
        cum = cum_r[rows, :]
        cum_t = jnp.transpose(cum)
        stepw = exact(step, spread)
        u = xc * stepw
        scores = mm(cc, b, NT)
        d_scores = jnp.zeros((Q, Q), f32)
        d_cum = jnp.zeros((Q, LANES), f32)
        cols = jnp.zeros((8, Q), f32)
        dus = []
        for g in range(inner // LANES):
            up = u[:, g * LANES : (g + 1) * LANES].astype(bf16)
            dyp = dy[:, g * LANES : (g + 1) * LANES]
            acc = jnp.zeros((Q, LANES), f32)
            for k in range(per):
                h = g * per + k
                e = jnp.exp(jnp.where(causal, cum[:, h : h + 1] - cum_t[h : h + 1, :], -1e30))
                p = scores * e
                dyh = jnp.where(lane // head_dim == k, dyp, 0.0).astype(bf16)
                dp = mm(dyh, up, NT)
                d_scores = d_scores + dp * e
                gp = dp * p
                d_cum = d_cum + jnp.where(lane == h, jnp.sum(gp, axis=1, keepdims=True), 0.0)
                cols = cols + jnp.where(
                    iota((8, Q), 0) == h, jnp.sum(gp, axis=0, keepdims=True), 0.0
                )
                acc = acc + mm(p, dyh, TN)
            dus.append(acc)
        du = jnp.concatenate(dus, axis=1)
        d_cum = d_cum - jnp.transpose(
            jnp.concatenate([cols, jnp.zeros((LANES - 8, Q), f32)], axis=0)
        )
        d_c = mm(d_scores, b)
        d_b = mm(d_scores, cc, TN)
        d_prev = None
        if c > 0:
            state = state_r[c]
            decayed = exact(jnp.exp(cum), spread)
            dz = dy * decayed
            carried = mm(cc, state, NT) * dz
            d_cum = d_cum + exact(carried, spread, NT)
            d_c = d_c + mm(dz, state)
            d_prev = mm(dz, cc, TN)
        if d_state is not None:
            last = cum[Q - 1 : Q, :]
            tailw = exact(jnp.exp(last - cum), spread)
            ut = u * tailw
            dut = mm(b, d_state, NT)
            d_b = d_b + mm(ut, d_state)
            du = du + dut * tailw
            q = exact(dut * ut, spread, NT)
            d_last = jnp.sum(q, axis=0, keepdims=True)
            if c > 0:
                rowdec = jnp.sum(spread_r * jnp.exp(last), axis=1, keepdims=True)
                r = jnp.sum(d_state * state_r[c], axis=1, keepdims=True) * rowdec
                d_last = d_last + jnp.sum(spread_r * r, axis=0, keepdims=True)
                d_prev = d_prev + d_state * rowdec
            d_cum = d_cum - q + jnp.where(iota((Q, LANES), 0) == Q - 1, d_last, 0.0)
        d_state = d_prev
        d_log = exact(lower, d_cum, TN)
        g_alog = g_alog + jnp.sum(d_log * log_decay, axis=0, keepdims=True)
        d_step = exact(du * xc, spread, NT) - d_log * rate
        d_pre = d_step * jax.nn.sigmoid(pre)
        d_pre = jnp.where(lane < heads, d_pre, 0.0)
        g_dtb = g_dtb + jnp.sum(d_pre, axis=0, keepdims=True)
        g_skip = g_skip + jnp.sum(dy * xc, axis=0, keepdims=True)
        dxc = du * stepw + skip * dy
        dvx = dxc * (sx * (1.0 + vx * (1.0 - sx)))
        dvb = jnp.concatenate([d_b, d_c], axis=1) * (sb * (1.0 + vb * (1.0 - sb)))
        dvx_s[rows, :] = dvx
        dvbc_s[rows, :] = dvb
        g_cxb = g_cxb + jnp.sum(dvx, axis=0, keepdims=True)
        g_cbcb = g_cbcb + jnp.sum(dvb, axis=0, keepdims=True)
        dx = jnp.zeros((Q, inner), f32)
        dbc = jnp.zeros((Q, 2 * states), f32)
        for j in range(taps):
            back = pl.ds(c * Q + taps - 1 - j, Q)
            ahead = pl.ds(HEAD + c * Q - taps + 1 + j, Q)
            dx = dx + cx[j : j + 1, :] * dvx_s[back, :]
            dbc = dbc + cbc[j : j + 1, :] * dvbc_s[back, :]
            g_cx[j] = g_cx[j] + jnp.sum(dvx * x_r[ahead, :], axis=0, keepdims=True)
            g_cbc[j] = g_cbc[j] + jnp.sum(dvb * bc_r[ahead, :], axis=0, keepdims=True)
        dx_s[rows, :] = dx.astype(bf16)
        dbd_s[rows, :] = jnp.concatenate([dbc, d_pre], axis=1).astype(bf16)

    g_ng = jnp.zeros((1, tok.shape[1]), f32)
    for c in range(chunks):
        rows = pl.ds(c * Q, Q)
        res_o[rows, :] = mm(gn_s[rows, :], wo[...]).astype(bf16)
        dn = mm(dz_s[rows, :], wz[...], NT) + mm(dx_s[rows, :], wx[...], NT)
        dn = dn + mm(dbd_s[rows, :], wbd[...], NT)
        dn_o[rows, :] = dn.astype(bf16)
        t = tok[rows, :].astype(f32)
        unit = t * lax.rsqrt(jnp.mean(t * t, axis=-1, keepdims=True) + epsilon)
        g_ng = g_ng + jnp.sum(dn * unit, axis=0, keepdims=True)
    gz_o[...] = mm(normed[...], dz_s[...], TN).astype(bf16)
    gx_o[...] = mm(normed[...], dx_s[...], TN).astype(bf16)
    gwo_o[...] = mm(gn_s[...], cot[...], TN).astype(bf16)
    gb = mm(normed[...], dbd_s[:, : 2 * states], TN).astype(bf16)
    width = gb.shape[0]
    for k in range(2 * states // LANES):
        gbc_o[pl.ds(k * width, width), :] = gb[:, k * LANES : (k + 1) * LANES]
    gdt = mm(dbd_s[:, 2 * states :], normed[...], TN)
    sm_o[...] = jnp.zeros(sm_o.shape, f32)
    smt_o[...] = jnp.zeros(smt_o.shape, f32)
    at = put_rows(sm_o, 0, gdt[0:heads, :])
    for row in (*g_cx, g_cxb, g_gain):
        at = put_rows(sm_o, at, row)
    for row in (g_dtb, g_alog, exact(g_skip, spread, NT)):
        at = put_rows(sm_o, at, row)
    at = 0
    for row in (*g_cbc, g_cbcb, g_ng):
        at = put_rows(smt_o, at, row)


class Stream:
    def __init__(self, src, bits):
        rows, self.lanes = src.shape
        self.rows, self.dtype, self.bits = rows, src.dtype, bits
        tile = 32 // jnp.dtype(src.dtype).itemsize
        self.halve = []
        for _ in bits:
            split = rows % (2 * tile) == 0
            self.halve.append(split)
            if split:
                rows //= 2
        self.copies = len(bits) + sum(self.halve)

    def scratch(self):
        rows, shapes = self.rows, []
        shapes.append(pltpu.VMEM((self.rows, self.lanes), self.dtype))
        shapes.append(pltpu.VMEM((self.rows, self.lanes), self.dtype))
        shapes.append(pltpu.SemaphoreType.DMA((self.copies,)))
        shapes.append(pltpu.SemaphoreType.DMA((self.copies,)))
        for split in self.halve:
            if split:
                rows //= 2
            shapes.append(pltpu.VMEM((rows, self.lanes), self.dtype))
        return shapes


def run_stream(stream, src, refs):
    acc, out, send, recv = refs[:4]
    slots = refs[4:]
    off, size, ref = 0, stream.rows, src
    trail = []
    sem = 0
    tile = 32 // jnp.dtype(stream.dtype).itemsize

    def place(v):
        return v if isinstance(v, int) else pl.multiple_of(v, tile)

    last = len(stream.bits) - 1
    for k, ((axis, bit), split) in enumerate(zip(stream.bits, stream.halve)):
        me = lax.axis_index(axis)
        side = lax.rem(me // bit, 2)
        peer = me + bit - 2 * bit * side
        if split:
            half = size // 2
            keep, give = off + side * half, off + (1 - side) * half
            trail.append((axis, peer, off))
        else:
            half, keep, give = size, off, off
        copy = pltpu.make_async_remote_copy(
            src_ref=ref.at[pl.ds(place(give), half), :],
            dst_ref=slots[k],
            send_sem=send.at[sem],
            recv_sem=recv.at[sem],
            device_id={axis: peer},
            device_id_type=pl.DeviceIdType.MESH,
        )
        sem += 1
        copy.start()
        yield
        copy.wait()
        rows = pl.ds(place(keep), half)
        target = out if k == last else acc
        total = ref[rows, :].astype(f32) + slots[k][...].astype(f32)
        target[rows, :] = total.astype(stream.dtype)
        off, size, ref = keep, half, target
    for axis, peer, parent in reversed(trail):
        rows = pl.ds(place(off), size)
        copy = pltpu.make_async_remote_copy(
            src_ref=out.at[rows, :],
            dst_ref=out.at[rows, :],
            send_sem=send.at[sem],
            recv_sem=recv.at[sem],
            device_id={axis: peer},
            device_id_type=pl.DeviceIdType.MESH,
        )
        sem += 1
        copy.start()
        yield
        copy.wait()
        off, size = parent, size * 2


def greet(peers):
    barrier = pltpu.get_barrier_semaphore()
    for axis, bit in peers:
        me = lax.axis_index(axis)
        peer = me + bit - 2 * bit * lax.rem(me // bit, 2)
        pl.semaphore_signal(
            barrier, inc=1, device_id={axis: peer}, device_id_type=pl.DeviceIdType.MESH
        )
    pl.semaphore_wait(barrier, len(peers))


def run_all(streams, sources, scratch):
    running = []
    at = 0
    outs = []
    for stream, src in zip(streams, sources):
        count = 4 + len(stream.bits)
        refs = scratch[at : at + count]
        at += count
        outs.append(refs[1])
        running.append(run_stream(stream, src, refs))
    while running:
        running = [r for r in running if next(r, 1) is None]
    return outs


def kernel_stats(streams, peers, src, out, *scratch):
    greet(peers)
    (total,) = run_all(streams, [src], scratch)
    out[...] = total[...]


def kernel_sums(
    streams, peers, tok, cot, ng, res, dn, gz, gx, gwo, gbc, sm, smt,
    res_o, gt_o, gz_o, gx_o, gwo_o, gbc_o, sm_o, smt_o, *scratch,
):
    greet(peers)
    a_res, a_dn, a_gz, a_gx, a_gwo, a_gbc, a_sm, a_smt = run_all(
        streams, [res, dn, gz, gx, gwo, gbc, sm, smt], scratch
    )
    for c in range(tok.shape[0] // Q):
        rows = pl.ds(c * Q, Q)
        t = tok[rows, :].astype(f32)
        res_o[rows, :] = (t + a_res[rows, :].astype(f32)).astype(bf16)
        r = lax.rsqrt(jnp.mean(t * t, axis=-1, keepdims=True) + epsilon)
        gd = a_dn[rows, :].astype(f32) * ng[...]
        mean = jnp.mean(t * gd, axis=-1, keepdims=True)
        d = r * gd - t * (r * r * r) * mean
        gt_o[rows, :] = (cot[rows, :].astype(f32) + d).astype(bf16)
    gz_o[...] = a_gz[...].astype(f32)
    gx_o[...] = a_gx[...].astype(f32)
    gwo_o[...] = a_gwo[...].astype(f32)
    width = gbc_o.shape[0]
    for k in range(gbc_o.shape[1] // LANES):
        gbc_o[:, k * LANES : (k + 1) * LANES] = a_gbc[pl.ds(k * width, width), :].astype(f32)
    sm_o[...] = a_sm[...]
    smt_o[...] = a_smt[...]


def call(body, args, outs, scratch=(), **params):
    vmem = pl.BlockSpec(memory_space=pltpu.VMEM)
    return pl.pallas_call(
        body,
        out_shape=[jax.ShapeDtypeStruct(s, d) for s, d in outs],
        in_specs=[vmem] * len(args),
        out_specs=[vmem] * len(outs),
        scratch_shapes=list(scratch),
        compiler_params=pltpu.CompilerParams(vmem_limit_bytes=60 * 1024 * 1024, **params),
    )(*args)


def per_device(
    tokens, cotangent, norm_gain, w_z, w_x, w_bc, w_dt, conv_x, conv_x_bias, conv_bc,
    conv_bc_bias, dt_bias, a_log, d_skip, gate_gain, w_out,
):
    seqs, length, width = tokens.shape
    assert seqs == 1 and length % Q == 0
    heads = dt_bias.shape[0]
    inner = w_z.shape[1]
    wide = w_bc.shape[1]
    states = wide // 2
    taps = conv_x.shape[0]
    dp, tensor = lax.axis_size("dp"), lax.axis_size("tensor")
    inner_total = inner * tensor
    chunks = length // Q
    tok = tokens.reshape(length, width)
    cot = cotangent.reshape(length, width)
    wbd = jnp.concatenate([w_bc, jnp.pad(w_dt, ((0, 0), (0, LANES - heads)))], axis=1)
    hp = jnp.pad(jnp.stack([dt_bias, a_log, d_skip]), ((0, 5), (0, LANES - heads)))
    shared = (
        tok, cot, norm_gain[None, :], w_z, w_x, wbd, conv_x, conv_x_bias[None, :], conv_bc,
        conv_bc_bias[None, :], hp, gate_gain[None, :], w_out,
    )
    kept = call(
        functools.partial(kernel_front, heads),
        shared,
        [
            ((length, width), bf16),
            ((length, inner), f32),
            ((length + HEAD, inner), f32),
            ((length + HEAD, wide), f32),
            ((length, LANES), f32),
            ((length, LANES), f32),
            ((chunks, inner, states), f32),
            ((length, inner), f32),
            ((length, inner), f32),
            ((8, length), f32),
        ],
    )
    t_bits = [("tensor", 1 << k) for k in range(tensor.bit_length() - 1)]
    d_bits = [("dp", 1 << k) for k in range(dp.bit_length() - 1)]
    stats = kept[-1]
    stream = Stream(stats, t_bits)
    (stats,) = call(
        functools.partial(kernel_stats, [stream], t_bits),
        (stats,),
        [(stats.shape, f32)],
        stream.scratch(),
        collective_id=0,
        has_side_effects=True,
    )
    sm_rows = heads * width // LANES + (taps + 2) * inner // LANES + 3
    unit = 8 * dp
    sm_rows = -(-sm_rows // unit) * unit
    smt_rows = (taps + 1) * wide // LANES + width // LANES
    smt_rows = -(-smt_rows // 16) * 16
    parts = call(
        functools.partial(kernel_back, heads, inner_total),
        (*shared, *kept[:-1], stats),
        [
            ((length, width), bf16),
            ((length, width), bf16),
            ((width, inner), bf16),
            ((width, inner), bf16),
            ((inner, width), bf16),
            ((width * wide // LANES, LANES), bf16),
            ((sm_rows, LANES), f32),
            ((smt_rows, LANES), f32),
        ],
        [
            pltpu.VMEM((length, inner), bf16),
            pltpu.VMEM((length, inner), bf16),
            pltpu.VMEM((length, inner), bf16),
            pltpu.VMEM((length, wide + LANES), bf16),
            pltpu.VMEM((length + HEAD, inner), f32),
            pltpu.VMEM((length + HEAD, wide), f32),
            pltpu.VMEM((length, LANES), f32),
        ],
    )
    turned = d_bits[1:2] + d_bits[:1] + d_bits[2:]
    bits = [t_bits, t_bits, turned, d_bits, d_bits, t_bits + d_bits, d_bits, t_bits + d_bits]
    streams = [Stream(part, b) for part, b in zip(parts, bits)]
    result, grad_x, gz, gx, gwo, gbc, sm, smt = call(
        functools.partial(kernel_sums, streams, t_bits + d_bits),
        (tok, cot, norm_gain[None, :], *parts),
        [
            ((length, width), bf16),
            ((length, width), bf16),
            ((width, inner), f32),
            ((width, inner), f32),
            ((inner, width), f32),
            ((width, wide), f32),
            ((sm_rows, LANES), f32),
            ((smt_rows, LANES), f32),
        ],
        [shape for s in streams for shape in s.scratch()],
        collective_id=1,
        has_side_effects=True,
    )
    sizes = [heads * width, taps * inner, inner, inner, LANES, LANES, LANES]
    flat, at, cut = sm.reshape(-1), 0, []
    for size in sizes:
        cut.append(flat[at : at + size])
        at += size
    gdt, g_cx, g_cxb, g_gain, g_dtb, g_alog, g_skip = cut
    flat, at, cut = smt.reshape(-1), 0, []
    for size in (taps * wide, wide, width):
        cut.append(flat[at : at + size])
        at += size
    g_cbc, g_cbcb, g_ng = cut
    return (
        result.reshape(seqs, length, width),
        grad_x.reshape(seqs, length, width),
        g_ng,
        gz,
        gx,
        gbc,
        gdt.reshape(heads, width).T,
        g_cx.reshape(taps, inner),
        g_cxb,
        g_cbc.reshape(taps, wide),
        g_cbcb,
        g_dtb[:heads],
        g_alog[:heads],
        g_skip[:heads],
        g_gain,
        gwo,
    )


def solution(mesh):
    placed = (
        P("dp", None, None),
        P("dp", None, None),
        P(),
        P(None, "tensor"),
        P(None, "tensor"),
        P(),
        P(None, "tensor"),
        P(None, "tensor"),
        P("tensor"),
        P(),
        P(),
        P("tensor"),
        P("tensor"),
        P("tensor"),
        P("tensor"),
        P("tensor", None),
    )
    return jax.shard_map(
        per_device,
        mesh=mesh,
        in_specs=placed,
        out_specs=(
            P("dp", None, None),
            P("dp", None, None),
            P(),
            P(None, "tensor"),
            P(None, "tensor"),
            P(),
            P(None, "tensor"),
            P(None, "tensor"),
            P("tensor"),
            P(),
            P(),
            P("tensor"),
            P("tensor"),
            P("tensor"),
            P("tensor"),
            P("tensor", None),
        ),
        check_vma=False,
    )
```

time: 585 us -> 134 us (0.23)
  waiting for transfers between devices: 229 us -> 0 us
  Pallas kernels: 0 us -> 106 us
  local copies, waits for them, and re-layouts: 118 us -> 23.2 us
  blocking collectives: 90.8 us -> 0 us
  other arithmetic: 71.2 us -> 3.17 us
  matrix products: 55.8 us -> 0 us
  between operations: 14.7 us -> 0.69 us
    psum x3 -> x0, waiting for transfers between devices: 229 us -> none  [the longest x1 143 us: per_device(): lax.psum((grad_w_z, grad_w_x, grad_w_dt, back[3], back[4], back[7], back[...]
    pallas_call x0 -> x4, Pallas kernels: none -> 106 us  [call(): pl.pallas_call(body, out_shape=[jax.ShapeDtypeStruct(s, d) for s, d in ou...]
    psum x4 -> x0, blocking collectives: 90.8 us -> none  [the longest x1 38.6 us: per_device(): lax.psum((grad_w_z, grad_w_x, grad_w_dt, back[3], back[4], back[7], back[...]
    dot_general x39 -> x0, matrix products: 55.8 us -> none  [the longest x6 18.1 us: advance(): inside = jnp.einsum('tsh,shp->thp', mixing, x_blk, precision=highest)]
    dynamic_update_slice x26 -> x0, local copies, waits for them, and re-layouts: 44.2 us -> none  [state_scan(): _, outputs = lax.scan(advance, initial, pieces)]
    another operation x19 -> x1, other arithmetic: 26.8 us -> 1.29 us  [per_device(): jnp.stack([dt_bias, a_log, d_skip])]
    another operation x29 -> x0, local copies, waits for them, and re-layouts: 20.1 us -> none
    reduce_sum x15 -> x0, other arithmetic: 16.9 us -> none  [the longest x2 4.24 us: mixer(): mixed = mixed + d_skip[None, :, None] * xheads]
  transfers between devices with their start and end apart: 3 -> 0, of which waited for: 2 -> 0; matrix products, arithmetic and copies ran while one was open for 3% -> 0% of each run, Pallas kernels for 0% -> 0%
where the time goes in v1:
time: 134 us; the launch traced here: 133 us
  Pallas kernels  106 us (79%)
  local copies, waits for them, and re-layouts  23.2 us (17%)
  other arithmetic  3.17 us (2%)
    pallas_call x4, Pallas kernels, call(): pl.pallas_call(body, out_shape=[jax.ShapeDtypeStruct(s, d) for s, d in ou...  106 us
    unnamed x17, local copies, waits for them, and re-layouts  10.3 us
    slice x6, local copies, waits for them, and re-layouts, per_device(): cut.append(flat[at:at + size])  6.04 us

profile of v1, /device:TPU:0, one launch (start us, length us, event | category | flops | bytes accessed | tf_op | source)
XLA Modules:
  0.0 133.2 jit_solution(1715139060547114239)
XLA Ops:
  0.6 1.2 broadcast_in_dim.14.cxb
  1.9 1.2 broadcast_in_dim.16.gg
  3.1 1.3 broadcast_in_dim.13.ng
  4.4 1.3 select_maximum_fusion.hp
  5.7 0.9 copy.32
  6.6 1.9 %fusion.1.wbd = bf16[768,384]{1,0:T(8,128)(2,1)} fusion(bf16[768,6]{1,0:T(8,128)(2,1)S(1)} %copy.32, bf16[768,256]{1,0:T(8,128)(2,1)} %param.21), kind=kLoop, calls=%fused_computation.2 | loop fusion | flops 1769472 | bytes 992256 | tf_op jit(solution)/shard_map/concatenate | solution.py:498
  8.5 8.7 %shard_map.279 = (bf16[512,768]{1,0:T(8,128)(2,1)}, f32[512,384]{1,0:T(8,128)}, f32[520,384]{1,0:T(8,128)}, f32[520,256]{1,0:T(8,128)}, f32[512,128]{1,0:T(8,128...) custom-call(bf16[512,768]{1,0:T(8,128)(2,1)} %bitcast.23, ...), custom_call_target="tpu_custom_call" | custom-call | tf_op jit(solution)/shard_map/pallas_call | solution.py:472
  17.2 7.2 %shard_map.280.stats = f32[8,512]{1,0:T(8,128)} custom-call(f32[8,512]{1,0:T(8,128)} %get-tuple-element.51.src), custom_call_target="tpu_custom_call" | custom-call | tf_op jit(solution)/shard_map/pallas_call | solution.py:472
  24.4 15.9 %shard_map.281 = (bf16[512,768]{1,0:T(8,128)(2,1)}, bf16[512,768]{1,0:T(8,128)(2,1)}, bf16[768,384]{1,0:T(8,128)(2,1)}, bf16[768,384]{1,0:T(8,128)(2,1)}, bf16[3...) custom-call(bf16[512,768]{1,0:T(8,128)(2,1)} %bitcast.24, ...), custom_call_target="tpu_custom_call" | custom-call | tf_op jit(solution)/shard_map/pallas_call | solution.py:472
  40.4 74.3 %shard_map.282 = (bf16[512,768]{1,0:T(8,128)(2,1)}, bf16[512,768]{1,0:T(8,128)(2,1)}, f32[768,384]{1,0:T(8,128)}, f32[768,384]{1,0:T(8,128)}, f32[384,768]{1,0:T...) custom-call(bf16[512,768]{1,0:T(8,128)(2,1)} %bitcast.25, bf16[512,768]{1,0:T(8,128)(2,1)} %bitcast.28, ...), custom_call_target="tpu_custom_call" | custom-call | tf_op jit(solution)/shard_map/pallas_call | solution.py:472
  114.6 0.0 copy-start.4
  114.6 1.3 slice_bitcast_fusion.3
  115.9 1.3 slice_bitcast_fusion.4
  117.2 0.7 slice.69
  117.9 1.3 slice_bitcast_fusion
  119.2 0.6 reshape.77
  119.8 1.3 slice_bitcast_fusion.1
  121.1 0.7 slice.66
  121.8 0.7 slice.65
  122.5 0.6 reshape.76
  123.1 0.6 reshape.75
  123.7 2.1 %copy.39 = bf16[1,512,768]{2,1,0:T(8,128)(2,1)} copy(bf16[1,512,768]{2,1,0:T(8,128)(2,1)} %bitcast.30) | data formatting | bytes 1572864
  125.8 0.0 copy-done.4
  125.8 0.0 copy-start.2
  125.8 0.9 copy.40
  126.7 0.7 copy-done.2
  127.4 0.0 copy-start.1
  127.4 1.0 copy.41
  128.4 0.7 copy-done.1
  129.1 0.0 copy-start.3
  129.1 1.0 copy.42
  130.1 0.5 copy-done.3
  130.6 0.0 copy-start
  130.6 0.9 copy.43
  131.5 0.7 copy-done
  132.2 1.0 copy.44
Async XLA Ops:
  114.6 11.2 %copy-start.4 = (bf16[512,768]{1,0:T(8,128)(2,1)S(1)}, bf16[512,768]{1,0:T(8,128)(2,1)}, u32[]{:S(2)}) copy-start(bf16[512,768]{1,0:T(8,128)(2,1)} %get-tuple-element.61) | copy-start | bytes 2359300
  125.8 1.6 %copy-start.2 = (f32[768,384]{1,0:T(8,128)S(1)}, f32[768,384]{1,0:T(8,128)}, u32[]{:S(2)}) copy-start(f32[768,384]{1,0:T(8,128)} %get-tuple-element.92) | copy-start | bytes 3538948
  127.4 1.7 %copy-start.1 = (f32[768,384]{1,0:T(8,128)S(1)}, f32[768,384]{1,0:T(8,128)}, u32[]{:S(2)}) copy-start(f32[768,384]{1,0:T(8,128)} %get-tuple-element.93) | copy-start | bytes 3538948
  129.1 1.6 %copy-start.3 = (f32[768,256]{1,0:T(8,128)S(1)}, f32[768,256]{1,0:T(8,128)}, u32[]{:S(2)}) copy-start(f32[768,256]{1,0:T(8,128)} %get-tuple-element.94) | copy-start | bytes 2359300
  130.6 1.6 %copy-start = (f32[384,768]{1,0:T(8,128)S(1)}, f32[384,768]{1,0:T(8,128)}, u32[]{:S(2)}) copy-start(f32[384,768]{1,0:T(8,128)} %get-tuple-element.104) | copy-start | bytes 3538948

commit v2 on v1

--- a/solution.py
+++ b/solution.py
@@ -62,10 +62,37 @@
     return pre, step, rate, log_decay, exact(lower, log_decay)
 
 
+def lane_row(ref):
+    lane = iota((1, LANES), 1)
+    total = jnp.zeros((1, LANES), f32)
+    for h in range(ref.shape[0]):
+        total = jnp.where(lane == h, ref[h], total)
+    return total
+
+
+def setup(dtw, dtb, alog, skip, wdt_s, hp):
+    wdt_s[...] = jnp.zeros(wdt_s.shape, bf16)
+    wdt_s[0 : dtw.shape[0], :] = dtw[...]
+    hp[...] = jnp.zeros(hp.shape, f32)
+    for k, ref in enumerate((dtb, alog, skip)):
+        hp[k : k + 1, :] = lane_row(ref)
+
+
+class Row:
+    def __init__(self, ref):
+        self.ref = ref
+
+    def __getitem__(self, index):
+        return self.ref[...][None, :]
+
+
 def kernel_front(
-    heads, tok, cot, ng, wz, wx, wbd, cx, cxb, cbc, cbcb, hp, gg, wo,
+    heads, tok, cot, ng, wz, wx, wbc, dtw, cx, cxb, cbc, cbcb, dtb, alog, dskip, gg, wo,
     normed_o, gate_o, x_o, bc_o, dt_o, cum_o, state_o, mixed_o, dgn_o, stats_o,
+    wdt_s, hp,
 ):
+    setup(dtw, dtb, alog, dskip, wdt_s, hp)
+    ng, cxb, cbcb, gg = Row(ng), Row(cxb), Row(cbcb), Row(gg)
     length, inner = mixed_o.shape
     states = cbc.shape[1] // 2
     head_dim = inner // heads
@@ -84,9 +111,8 @@
         normed_o[rows, :] = n
         gate_o[rows, :] = mm(n, wz[...])
         x_o[pl.ds(HEAD + c * Q, Q), :] = mm(n, wx[...])
-        bd = mm(n, wbd[...])
-        bc_o[pl.ds(HEAD + c * Q, Q), :] = bd[:, : 2 * states]
-        dt_o[rows, :] = bd[:, 2 * states :]
+        bc_o[pl.ds(HEAD + c * Q, Q), :] = mm(n, wbc[...])
+        dt_o[rows, :] = mm(n, wdt_s[...], NT)
         dgn_o[rows, :] = mm(cot[rows, :], wo[...], NT)
     state_o[0] = jnp.zeros((inner, states), f32)
     for c in range(chunks):
@@ -150,11 +176,13 @@
 
 
 def kernel_back(
-    heads, inner_total, tok, cot, ng, wz, wx, wbd, cx, cxb, cbc, cbcb, hp, gg, wo,
+    heads, inner_total, tok, cot, ng, wz, wx, wbc, dtw, cx, cxb, cbc, cbcb, dtb, alog, dskip, gg, wo,
     normed, gate_r, x_r, bc_r, dt_r, cum_r, state_r, mixed_r, dgn_r, stats,
     res_o, dn_o, gz_o, gx_o, gwo_o, gbc_o, sm_o, smt_o,
-    gn_s, dz_s, dx_s, dbd_s, dvx_s, dvbc_s, inv_s,
+    gn_s, dz_s, dx_s, dbc_s, ddt_s, dvx_s, dvbc_s, inv_s, wdt_s, hp,
 ):
+    setup(dtw, dtb, alog, dskip, wdt_s, hp)
+    cxb, cbcb, gg = Row(cxb), Row(cbcb), Row(gg)
     length, inner = mixed_r.shape
     states = cbc.shape[1] // 2
     head_dim = inner // heads
@@ -294,26 +322,29 @@
             g_cx[j] = g_cx[j] + jnp.sum(dvx * x_r[ahead, :], axis=0, keepdims=True)
             g_cbc[j] = g_cbc[j] + jnp.sum(dvb * bc_r[ahead, :], axis=0, keepdims=True)
         dx_s[rows, :] = dx.astype(bf16)
-        dbd_s[rows, :] = jnp.concatenate([dbc, d_pre], axis=1).astype(bf16)
+        dbc_s[rows, :] = dbc.astype(bf16)
+        ddt_s[rows, :] = d_pre.astype(bf16)
 
     g_ng = jnp.zeros((1, tok.shape[1]), f32)
     for c in range(chunks):
         rows = pl.ds(c * Q, Q)
         res_o[rows, :] = mm(gn_s[rows, :], wo[...]).astype(bf16)
         dn = mm(dz_s[rows, :], wz[...], NT) + mm(dx_s[rows, :], wx[...], NT)
-        dn = dn + mm(dbd_s[rows, :], wbd[...], NT)
+        dn = dn + mm(dbc_s[rows, :], wbc[...], NT) + mm(ddt_s[rows, :], wdt_s[...])
         dn_o[rows, :] = dn.astype(bf16)
         t = tok[rows, :].astype(f32)
         unit = t * lax.rsqrt(jnp.mean(t * t, axis=-1, keepdims=True) + epsilon)
         g_ng = g_ng + jnp.sum(dn * unit, axis=0, keepdims=True)
     gz_o[...] = mm(normed[...], dz_s[...], TN).astype(bf16)
     gx_o[...] = mm(normed[...], dx_s[...], TN).astype(bf16)
-    gwo_o[...] = mm(gn_s[...], cot[...], TN).astype(bf16)
-    gb = mm(normed[...], dbd_s[:, : 2 * states], TN).astype(bf16)
+    gw = mm(gn_s[...], cot[...], TN).astype(bf16)
+    for k in range(gw.shape[1] // inner):
+        gwo_o[pl.ds(k * inner, inner), :] = gw[:, k * inner : (k + 1) * inner]
+    gb = mm(normed[...], dbc_s[...], TN).astype(bf16)
     width = gb.shape[0]
     for k in range(2 * states // LANES):
         gbc_o[pl.ds(k * width, width), :] = gb[:, k * LANES : (k + 1) * LANES]
-    gdt = mm(dbd_s[:, 2 * states :], normed[...], TN)
+    gdt = mm(ddt_s[...], normed[...], TN)
     sm_o[...] = jnp.zeros(sm_o.shape, f32)
     smt_o[...] = jnp.zeros(smt_o.shape, f32)
     at = put_rows(sm_o, 0, gdt[0:heads, :])
@@ -327,8 +358,9 @@
 
 
 class Stream:
-    def __init__(self, src, bits):
-        rows, self.lanes = src.shape
+    def __init__(self, src, bits, start=0, rows=None, delay=0):
+        self.start, self.delay = start, delay
+        rows, self.lanes = rows or src.shape[0], src.shape[1]
         self.rows, self.dtype, self.bits = rows, src.dtype, bits
         tile = 32 // jnp.dtype(src.dtype).itemsize
         self.halve = []
@@ -355,6 +387,7 @@
 def run_stream(stream, src, refs):
     acc, out, send, recv = refs[:4]
     slots = refs[4:]
+    src = src.at[pl.ds(stream.start, stream.rows), :]
     off, size, ref = 0, stream.rows, src
     trail = []
     sem = 0
@@ -429,25 +462,67 @@
         at += count
         outs.append(refs[1])
         running.append(run_stream(stream, src, refs))
-    while running:
-        running = [r for r in running if next(r, 1) is None]
+    for r in running:
+        next(r)
+    tick = 0
+    pending = list(zip(running, (s.delay for s in streams)))
+    while pending:
+        pending = [(r, d) for r, d in pending if tick < d or next(r, 1) is None]
+        tick += 1
     return outs
 
 
-def kernel_stats(streams, peers, src, out, *scratch):
+def kernel_stats(axis, src, out, slots, send, recv):
+    size = lax.axis_size(axis)
+    me = lax.axis_index(axis)
+    barrier = pltpu.get_barrier_semaphore()
+    for d in range(1, size):
+        pl.semaphore_signal(
+            barrier,
+            inc=1,
+            device_id={axis: lax.rem(me + d, size)},
+            device_id_type=pl.DeviceIdType.MESH,
+        )
+    pl.semaphore_wait(barrier, size - 1)
+    copies = []
+    for d in range(1, size):
+        copy = pltpu.make_async_remote_copy(
+            src_ref=src,
+            dst_ref=slots.at[d - 1],
+            send_sem=send.at[d - 1],
+            recv_sem=recv.at[d - 1],
+            device_id={axis: lax.rem(me + d, size)},
+            device_id_type=pl.DeviceIdType.MESH,
+        )
+        copy.start()
+        copies.append(copy)
+    total = src[...]
+    for d, copy in enumerate(copies):
+        copy.wait()
+        total = total + slots[d]
+    out[...] = total
+
+
+def kernel_sums(streams, sources, peers, *refs):
+    count = max(sources) + 1
+    srcs, outs, scratch = refs[:count], refs[count : 2 * count], refs[2 * count :]
     greet(peers)
-    (total,) = run_all(streams, [src], scratch)
-    out[...] = total[...]
-
-
-def kernel_sums(
-    streams, peers, tok, cot, ng, res, dn, gz, gx, gwo, gbc, sm, smt,
-    res_o, gt_o, gz_o, gx_o, gwo_o, gbc_o, sm_o, smt_o, *scratch,
+    gathered = run_all(streams, [srcs[k] for k in sources], scratch)
+    for stream, k, value in zip(streams, sources, gathered):
+        outs[k][pl.ds(stream.start, stream.rows), :] = value[...]
+
+
+def get_row(ref, at, width):
+    count = width // LANES
+    return jnp.concatenate([ref[at + k : at + k + 1, :] for k in range(count)], axis=1)
+
+
+def kernel_finish(
+    tok, cot, ng, a_res, a_dn, a_gz, a_gx, a_gwo, a_gbc, a_sm, a_smt,
+    res_o, gt_o, ng_o, gz_o, gx_o, gbc_o, gdt_o, cx_o, cxb_o, cbc_o, cbcb_o,
+    dtb_o, alog_o, skip_o, gain_o, gwo_o,
 ):
-    greet(peers)
-    a_res, a_dn, a_gz, a_gx, a_gwo, a_gbc, a_sm, a_smt = run_all(
-        streams, [res, dn, gz, gx, gwo, gbc, sm, smt], scratch
-    )
+    ng = Row(ng)
     for c in range(tok.shape[0] // Q):
         rows = pl.ds(c * Q, Q)
         t = tok[rows, :].astype(f32)
@@ -459,23 +534,42 @@
         gt_o[rows, :] = (cot[rows, :].astype(f32) + d).astype(bf16)
     gz_o[...] = a_gz[...].astype(f32)
     gx_o[...] = a_gx[...].astype(f32)
-    gwo_o[...] = a_gwo[...].astype(f32)
+    inner = gwo_o.shape[0]
+    for k in range(gwo_o.shape[1] // inner):
+        gwo_o[:, k * inner : (k + 1) * inner] = a_gwo[pl.ds(k * inner, inner), :].astype(f32)
     width = gbc_o.shape[0]
     for k in range(gbc_o.shape[1] // LANES):
         gbc_o[:, k * LANES : (k + 1) * LANES] = a_gbc[pl.ds(k * width, width), :].astype(f32)
-    sm_o[...] = a_sm[...]
-    smt_o[...] = a_smt[...]
-
-
-def call(body, args, outs, scratch=(), **params):
+    at = 0
+    for out in (gdt_o, cx_o):
+        for r in range(out.shape[0]):
+            out[r : r + 1, :] = get_row(a_sm, at, out.shape[1])
+            at += out.shape[1] // LANES
+    for out in (cxb_o, gain_o):
+        out[...] = get_row(a_sm, at, out.shape[0])[0]
+        at += out.shape[0] // LANES
+    for out in (dtb_o, alog_o, skip_o):
+        out[...] = a_sm[at, 0 : out.shape[0]]
+        at += 1
+    at = 0
+    for r in range(cbc_o.shape[0]):
+        cbc_o[r : r + 1, :] = get_row(a_smt, at, cbc_o.shape[1])
+        at += cbc_o.shape[1] // LANES
+    for out in (cbcb_o, ng_o):
+        out[...] = get_row(a_smt, at, out.shape[0])[0]
+        at += out.shape[0] // LANES
+
+
+def call(body, args, outs, scratch=(), limit=40, **params):
     vmem = pl.BlockSpec(memory_space=pltpu.VMEM)
+    smem = pl.BlockSpec(memory_space=pltpu.SMEM)
     return pl.pallas_call(
         body,
         out_shape=[jax.ShapeDtypeStruct(s, d) for s, d in outs],
-        in_specs=[vmem] * len(args),
+        in_specs=[smem if a.ndim == 1 and a.shape[0] < LANES else vmem for a in args],
         out_specs=[vmem] * len(outs),
         scratch_shapes=list(scratch),
-        compiler_params=pltpu.CompilerParams(vmem_limit_bytes=60 * 1024 * 1024, **params),
+        compiler_params=pltpu.CompilerParams(vmem_limit_bytes=limit * 1024 * 1024, **params),
     )(*args)
 
 
@@ -495,12 +589,11 @@
     chunks = length // Q
     tok = tokens.reshape(length, width)
     cot = cotangent.reshape(length, width)
-    wbd = jnp.concatenate([w_bc, jnp.pad(w_dt, ((0, 0), (0, LANES - heads)))], axis=1)
-    hp = jnp.pad(jnp.stack([dt_bias, a_log, d_skip]), ((0, 5), (0, LANES - heads)))
     shared = (
-        tok, cot, norm_gain[None, :], w_z, w_x, wbd, conv_x, conv_x_bias[None, :], conv_bc,
-        conv_bc_bias[None, :], hp, gate_gain[None, :], w_out,
-    )
+        tok, cot, norm_gain, w_z, w_x, w_bc, w_dt.T, conv_x, conv_x_bias, conv_bc,
+        conv_bc_bias, dt_bias, a_log, d_skip, gate_gain, w_out,
+    )
+    own = [pltpu.VMEM((LANES, width), bf16), pltpu.VMEM((8, LANES), f32)]
     kept = call(
         functools.partial(kernel_front, heads),
         shared,
@@ -516,16 +609,21 @@
             ((length, inner), f32),
             ((8, length), f32),
         ],
+        own,
     )
     t_bits = [("tensor", 1 << k) for k in range(tensor.bit_length() - 1)]
     d_bits = [("dp", 1 << k) for k in range(dp.bit_length() - 1)]
     stats = kept[-1]
-    stream = Stream(stats, t_bits)
     (stats,) = call(
-        functools.partial(kernel_stats, [stream], t_bits),
+        functools.partial(kernel_stats, "tensor"),
         (stats,),
         [(stats.shape, f32)],
-        stream.scratch(),
+        [
+            pltpu.VMEM((tensor - 1, *stats.shape), f32),
+            pltpu.SemaphoreType.DMA((tensor - 1,)),
+            pltpu.SemaphoreType.DMA((tensor - 1,)),
+        ],
+        limit=4,
         collective_id=0,
         has_side_effects=True,
     )
@@ -542,7 +640,7 @@
             ((length, width), bf16),
             ((width, inner), bf16),
             ((width, inner), bf16),
-            ((inner, width), bf16),
+            ((width, inner), bf16),
             ((width * wide // LANES, LANES), bf16),
             ((sm_rows, LANES), f32),
             ((smt_rows, LANES), f32),
@@ -551,61 +649,66 @@
             pltpu.VMEM((length, inner), bf16),
             pltpu.VMEM((length, inner), bf16),
             pltpu.VMEM((length, inner), bf16),
-            pltpu.VMEM((length, wide + LANES), bf16),
+            pltpu.VMEM((length, wide), bf16),
+            pltpu.VMEM((length, LANES), bf16),
             pltpu.VMEM((length + HEAD, inner), f32),
             pltpu.VMEM((length + HEAD, wide), f32),
             pltpu.VMEM((length, LANES), f32),
+            *own,
         ],
     )
     turned = d_bits[1:2] + d_bits[:1] + d_bits[2:]
-    bits = [t_bits, t_bits, turned, d_bits, d_bits, t_bits + d_bits, d_bits, t_bits + d_bits]
-    streams = [Stream(part, b) for part, b in zip(parts, bits)]
-    result, grad_x, gz, gx, gwo, gbc, sm, smt = call(
-        functools.partial(kernel_sums, streams, t_bits + d_bits),
-        (tok, cot, norm_gain[None, :], *parts),
+    res, dn, gz, gx, gwo, gbc, sm, smt = parts
+    half = width // 2
+    plan = [
+        (7, Stream(smt, t_bits + d_bits)),
+        (5, Stream(gbc, t_bits + d_bits)),
+        (6, Stream(sm, d_bits)),
+        (2, Stream(gz, d_bits, 0, half)),
+        (0, Stream(res, t_bits)),
+        (2, Stream(gz, d_bits, half, half, 1)),
+        (3, Stream(gx, d_bits, 0, half, 2)),
+        (1, Stream(dn, t_bits, delay=2)),
+        (3, Stream(gx, d_bits, half, half, 3)),
+        (4, Stream(gwo, d_bits, 0, half, 4)),
+        (4, Stream(gwo, turned, half, half, 4)),
+    ]
+    streams = [s for _, s in plan]
+    sums = call(
+        functools.partial(kernel_sums, streams, [k for k, _ in plan], t_bits + d_bits),
+        parts,
+        [(p.shape, p.dtype) for p in parts],
+        [shape for s in streams for shape in s.scratch()],
+        collective_id=1,
+        has_side_effects=True,
+    )
+    outs = call(
+        kernel_finish,
+        (tok, cot, norm_gain, *sums),
         [
             ((length, width), bf16),
             ((length, width), bf16),
+            ((width,), f32),
             ((width, inner), f32),
             ((width, inner), f32),
+            ((width, wide), f32),
+            ((heads, width), f32),
+            ((taps, inner), f32),
+            ((inner,), f32),
+            ((taps, wide), f32),
+            ((wide,), f32),
+            ((heads,), f32),
+            ((heads,), f32),
+            ((heads,), f32),
+            ((inner,), f32),
             ((inner, width), f32),
-            ((width, wide), f32),
-            ((sm_rows, LANES), f32),
-            ((smt_rows, LANES), f32),
         ],
-        [shape for s in streams for shape in s.scratch()],
-        collective_id=1,
-        has_side_effects=True,
-    )
-    sizes = [heads * width, taps * inner, inner, inner, LANES, LANES, LANES]
-    flat, at, cut = sm.reshape(-1), 0, []
-    for size in sizes:
-        cut.append(flat[at : at + size])
-        at += size
-    gdt, g_cx, g_cxb, g_gain, g_dtb, g_alog, g_skip = cut
-    flat, at, cut = smt.reshape(-1), 0, []
-    for size in (taps * wide, wide, width):
-        cut.append(flat[at : at + size])
-        at += size
-    g_cbc, g_cbcb, g_ng = cut
-    return (
-        result.reshape(seqs, length, width),
-        grad_x.reshape(seqs, length, width),
-        g_ng,
-        gz,
-        gx,
-        gbc,
-        gdt.reshape(heads, width).T,
-        g_cx.reshape(taps, inner),
-        g_cxb,
-        g_cbc.reshape(taps, wide),
-        g_cbcb,
-        g_dtb[:heads],
-        g_alog[:heads],
-        g_skip[:heads],
-        g_gain,
-        gwo,
-    )
+    )
+    outs = list(outs)
+    for k in range(2):
+        outs[k] = outs[k].reshape(seqs, length, width)
+    outs[6] = outs[6].T
+    return tuple(outs)
 
 
 def solution(mesh):

time: 134 us -> 101 us (0.75)
  Pallas kernels: 106 us -> 86.3 us
  local copies, waits for them, and re-layouts: 23.2 us -> 13.2 us
  other arithmetic: 3.17 us -> 0 us
    pallas_call x4 -> x5, Pallas kernels: 106 us -> 86.3 us  [call(): pl.pallas_call(body, out_shape=[jax.ShapeDtypeStruct(s, d) for s, d in ou...]
    slice x7 -> x0, local copies, waits for them, and re-layouts: 7.3 us -> none  [the longest x6 6.04 us: per_device(): cut.append(flat[at:at + size])]
    broadcast_in_dim x3 -> x0, local copies, waits for them, and re-layouts: 3.76 us -> none  [the longest x1 1.27 us: per_device(): norm_gain[None, :]]
    unnamed x17 -> x36, local copies, waits for them, and re-layouts: 10.3 us -> 13.2 us
    concatenate x1 -> x0, other arithmetic: 1.88 us -> none  [per_device(): jnp.concatenate([w_bc, jnp.pad(w_dt, ((0, 0), (0, LANES - heads)))], axis=1)]
    reshape x3 -> x0, local copies, waits for them, and re-layouts: 1.81 us -> none  [the longest x1 0.61 us: per_device(): gdt.reshape(heads, width)]
where the time goes in v2:
time: 101 us; the launch traced here: 100 us
  Pallas kernels  86.3 us (85%)
  local copies, waits for them, and re-layouts  13.2 us (13%)
    pallas_call x5, Pallas kernels, call(): pl.pallas_call(body, out_shape=[jax.ShapeDtypeStruct(s, d) for s, d in ou...  86.3 us
    unnamed x36, local copies, waits for them, and re-layouts  13.2 us

profile of v2, /device:TPU:0, one launch (start us, length us, event | category | flops | bytes accessed | tf_op | source)
XLA Modules:
  0.0 100.2 jit_solution(5918441970593401273)
XLA Ops:
  0.7 0.0 copy-start
  0.7 1.1 %copy-done = bf16[1,512,768]{2,1,0:T(8,128)(2,1)S(1)} copy-done((bf16[1,512,768]{2,1,0:T(8,128)(2,1)S(1)}, bf16[1,512,768]{2,1,0:T(8,128)(2,1)}, u32[]{:S(2)}) %copy-start) | copy-done | bytes 786456
  1.8 0.0 copy-start.2
  1.8 1.1 %copy-done.2 = bf16[1,512,768]{2,1,0:T(8,128)(2,1)S(1)} copy-done((bf16[1,512,768]{2,1,0:T(8,128)(2,1)S(1)}, bf16[1,512,768]{2,1,0:T(8,128)(2,1)}, u32[]{:S(2)}) %copy-start.2) | copy-done | bytes 786456
  2.9 0.0 copy-start.4
  2.9 1.1 %copy-done.4 = bf16[768,384]{1,0:T(8,128)(2,1)S(1)} copy-done((bf16[768,384]{1,0:T(8,128)(2,1)S(1)}, bf16[768,384]{1,0:T(8,128)(2,1)}, u32[]{:S(2)}) %copy-start.4) | copy-done | bytes 589848
  4.0 0.0 copy-start.5
  4.0 1.1 %copy-done.5 = bf16[768,384]{1,0:T(8,128)(2,1)S(1)} copy-done((bf16[768,384]{1,0:T(8,128)(2,1)S(1)}, bf16[768,384]{1,0:T(8,128)(2,1)}, u32[]{:S(2)}) %copy-start.5) | copy-done | bytes 589848
  5.1 0.0 copy-start.6
  5.1 1.1 %copy-done.6 = bf16[384,768]{1,0:T(8,128)(2,1)S(1)} copy-done((bf16[384,768]{1,0:T(8,128)(2,1)S(1)}, bf16[384,768]{1,0:T(8,128)(2,1)}, u32[]{:S(2)}) %copy-start.6) | copy-done | bytes 589848
  6.1 0.0 copy-start.7
  6.1 1.0 copy-done.7
  7.1 0.0 copy-start.8
  7.1 0.7 copy-done.8
  7.8 0.0 copy-start.9
  7.8 0.7 copy-done.9
  8.5 0.0 copy-start.10
  8.5 0.7 copy-done.10
  9.2 0.0 copy-start.11
  9.2 0.7 copy-done.11
  9.9 0.0 copy-start.12
  9.9 0.7 copy-done.12
  10.6 0.0 copy-start.13
  10.6 0.7 copy-done.13
  11.3 0.0 copy-start.14
  11.3 0.7 copy-done.14
  11.9 0.0 copy-start.15
  11.9 0.7 copy-done.15
  12.6 0.0 copy-start.16
  12.6 0.7 copy-done.16
  13.2 0.0 copy-start.17
  13.2 0.7 copy-done.17
  13.9 6.2 %shard_map.279 = (bf16[512,768]{1,0:T(8,128)(2,1)S(1)}, f32[512,384]{1,0:T(8,128)S(1)}, f32[520,384]{1,0:T(8,128)S(1)}, f32[520,256]{1,0:T(8,128)S(1)}, f32[512,...) custom-call(bf16[512,768]{1,0:T(8,128)(2,1)S(1)} %bitcast.6, ...), custom_call_target="tpu_custom_call" | custom-call | tf_op jit(solution)/shard_map/pallas_call | solution.py:566
  20.1 4.9 %shard_map.280.stats = f32[8,512]{1,0:T(8,128)S(1)} custom-call(f32[8,512]{1,0:T(8,128)S(1)} %get-tuple-element.67.src), custom_call_target="tpu_custom_call" | custom-call | tf_op jit(solution)/shard_map/pallas_call | solution.py:566
  25.0 12.3 %shard_map.281 = (bf16[512,768]{1,0:T(8,128)(2,1)S(1)}, bf16[512,768]{1,0:T(8,128)(2,1)S(1)}, bf16[768,384]{1,0:T(8,128)(2,1)S(1)}, bf16[768,384]{1,0:T(8,128)(2...) custom-call(bf16[512,768]{1,0:T(8,128)(2,1)S(1)} %bitcast.7, ...), custom_call_target="tpu_custom_call" | custom-call | tf_op jit(solution)/shard_map/pallas_call | solution.py:566
  37.2 0.0 copy-start.1
  37.3 0.0 copy-start.3
  37.3 59.5 %shard_map.282 = (bf16[512,768]{1,0:T(8,128)(2,1)S(1)}, bf16[512,768]{1,0:T(8,128)(2,1)S(1)}, bf16[768,384]{1,0:T(8,128)(2,1)S(1)}, bf16[768,384]{1,0:T(8,128)(2...) custom-call(bf16[512,768]{1,0:T(8,128)(2,1)S(1)} %get-tuple-element., ...), custom_call_target="tpu_custom_call" | custom-call | tf_op jit(solution)/shard_map/pallas_call | solution.py:566
  96.7 0.0 copy-done.1
  96.8 0.0 copy-done.3
  96.8 3.5 %shard_map.283 = (bf16[512,768]{1,0:T(8,128)(2,1)}, bf16[512,768]{1,0:T(8,128)(2,1)}, f32[768]{0:T(1024)}, f32[768,384]{1,0:T(8,128)}, f32[768,384]{1,0:T(8,128)...) custom-call(bf16[512,768]{1,0:T(8,128)(2,1)S(1)} %bitcast.8, ...), custom_call_target="tpu_custom_call" | custom-call | tf_op jit(solution)/shard_map/pallas_call | solution.py:566
Async XLA Ops:
  0.7 1.1 %copy-start = (bf16[1,512,768]{2,1,0:T(8,128)(2,1)S(1)}, bf16[1,512,768]{2,1,0:T(8,128)(2,1)}, u32[]{:S(2)}) copy-start(bf16[1,512,768]{2,1,0:T(8,128)(2,1)} %param.16) | copy-start | bytes 2359300
  1.8 1.1 %copy-start.2 = (bf16[1,512,768]{2,1,0:T(8,128)(2,1)S(1)}, bf16[1,512,768]{2,1,0:T(8,128)(2,1)}, u32[]{:S(2)}) copy-start(bf16[1,512,768]{2,1,0:T(8,128)(2,1)} %param.17) | copy-start | bytes 2359300
  2.9 1.1 %copy-start.4 = (bf16[768,384]{1,0:T(8,128)(2,1)S(1)}, bf16[768,384]{1,0:T(8,128)(2,1)}, u32[]{:S(2)}) copy-start(bf16[768,384]{1,0:T(8,128)(2,1)} %wz.3) | copy-start | bytes 1769476
  4.0 1.1 %copy-start.5 = (bf16[768,384]{1,0:T(8,128)(2,1)S(1)}, bf16[768,384]{1,0:T(8,128)(2,1)}, u32[]{:S(2)}) copy-start(bf16[768,384]{1,0:T(8,128)(2,1)} %wx.3) | copy-start | bytes 1769476
  5.1 1.1 %copy-start.6 = (bf16[384,768]{1,0:T(8,128)(2,1)S(1)}, bf16[384,768]{1,0:T(8,128)(2,1)}, u32[]{:S(2)}) copy-start(bf16[384,768]{1,0:T(8,128)(2,1)} %wo.3) | copy-start | bytes 1769476
  6.1 1.0 copy-start.7
  7.1 0.7 copy-start.8
  7.8 0.7 copy-start.9
  8.5 0.7 copy-start.10
  9.2 0.7 copy-start.11
  9.9 0.7 copy-start.12
  10.6 0.7 copy-start.13
  11.3 0.7 copy-start.14
  11.9 0.7 copy-start.15
  12.6 0.7 copy-start.16
  13.2 0.7 copy-start.17
  37.2 59.5 %copy-start.1 = (bf16[1,512,768]{2,1,0:T(8,128)(2,1)S(1)}, bf16[1,512,768]{2,1,0:T(8,128)(2,1)}, u32[]{:S(2)}) copy-start(bf16[1,512,768]{2,1,0:T(8,128)(2,1)} %param.16) | copy-start | bytes 2359300
  37.3 59.5 %copy-start.3 = (bf16[1,512,768]{2,1,0:T(8,128)(2,1)S(1)}, bf16[1,512,768]{2,1,0:T(8,128)(2,1)}, u32[]{:S(2)}) copy-start(bf16[1,512,768]{2,1,0:T(8,128)(2,1)} %param.17) | copy-start | bytes 2359300
